TPU v7x, 512 devices: a whole 4x4x16 slice. The times are simulated.
512 devices in a mesh: ctx: 64 (over x, z_lo, y), dp: 8 (over z_hi, core).
Axes of the slice: x: 4, y: 4, z: 16 (z_hi: 4, z_lo: 4; z = z_hi * 4 + z_lo), core: 2. Of those that a mesh axis runs over, the one named last changes fastest.
Arguments:
- layer_input: bfloat16 [16, 4096, 4096], P('dp', 'ctx'), may hold values from -1 to 1
- queries: bfloat16 [16, 4096, 1024], P('dp', 'ctx'), may hold values from -8 to 8
- key_states: bfloat16 [16, 4096, 128], P('dp', 'ctx'), may hold values from -8 to 8
- value_states: bfloat16 [16, 4096, 128], P('dp', 'ctx'), may hold values from -6 to 6
- attn_output: bfloat16 [16, 4096, 1024], P('dp', 'ctx'), may hold values from -6 to 6
- out_grad: bfloat16 [16, 4096, 1024], P('dp', 'ctx'), may hold values from -6 to 6
- doc_ids: int32 [16, 4096], P('dp'), may hold values from 0 to 15, never falling along the last dimension, each value on 1 to 1024 neighbouring positions
- positions: int32 [16, 4096], P('dp'), may hold values from 0 to 4095, as said below
Outputs:
- query_grad: bfloat16 [16, 4096, 1024], P('dp', 'ctx')
- kv_weight_grad: float32 [4096, 256], P('ctx')
Inputs may be any that keep to these rules, and one draw needn't show every extreme that they name: `positions`: stored row c * 64 + r of a sequence (c below 64, r below 64) holds a position from r * (64) to (r + 1) * 64 - 1; every position of a sequence is held by exactly one row.
All inputs are finite; a program needn't handle non-finite values.
Results may differ from a plain program's by a relative error of at most 0.005.
Values may be sent and summed in bfloat16 or wider, within the bound.
No kernel may reach another device: no remote copies, remote signals or barrier semaphores. Data moves between devices by JAX's collectives and lax.ppermute only.
A program may use at most 64 MiB of HBM per device.

v0:
```python
import math
import jax
import jax.numpy as jnp
from jax import lax
from jax.sharding import PartitionSpec as P

NEG_FILL = -1e30


def passed_along(x, axis, by):
    length = lax.axis_size(axis)
    return lax.ppermute(x, axis, [(i, (i + by) % length) for i in range(length)])


def heads_first(tensor, head_count):
    seq_count, row_count, width_all = tensor.shape
    head_size = width_all // head_count
    split_up = tensor.reshape(seq_count, row_count, head_count, head_size)
    return split_up.transpose(0, 2, 1, 3).reshape(seq_count, head_count * row_count, head_size)


def local(
    layer_input, queries, key_states, value_states, attn_output, out_grad, doc_ids, positions
):
    seq_count, row_count, model_width = layer_input.shape
    head_size = key_states.shape[2]
    head_count = queries.shape[2] // head_size
    ctx_count = lax.axis_size("ctx")
    ctx_index = lax.axis_index("ctx")
    score_scale = 1.0 / math.sqrt(head_size)
    query_n = heads_first(queries, head_count)
    grad_n = heads_first(out_grad, head_count)
    row_product = (out_grad.astype(jnp.float32) * attn_output.astype(jnp.float32)).reshape(
        seq_count, row_count, head_count, head_size
    )
    delta_n = (
        jnp.sum(row_product, axis=3).transpose(0, 2, 1).reshape(seq_count, head_count * row_count)
    )
    doc_full = jnp.take_along_axis(doc_ids, positions, axis=1)
    own_pos = lax.dynamic_slice_in_dim(positions, ctx_index * row_count, row_count, 1)
    own_doc = lax.dynamic_slice_in_dim(doc_full, ctx_index * row_count, row_count, 1)
    query_pos = jnp.tile(own_pos, (1, head_count))
    query_doc = jnp.tile(own_doc, (1, head_count))
    key_all, value_all = (
        lax.all_gather(key_states, "ctx", axis=1, tiled=True),
        lax.all_gather(value_states, "ctx", axis=1, tiled=True),
    )
    group_rows = 4 * row_count
    query_total = head_count * row_count

    def live_mask(key_doc, key_pos):
        return (key_doc[:, :, None] == query_doc[:, None, :]) & (
            key_pos[:, :, None] <= query_pos[:, None, :]
        )

    def scores_of(key_block):
        return (
            jnp.einsum("skd,snd->skn", key_block, query_n, preferred_element_type=jnp.float32)
            * score_scale
        )

    def stats_step(group_index, loop_state):
        run_max, run_sum = loop_state
        row_start = group_index * group_rows
        key_block = lax.dynamic_slice_in_dim(key_all, row_start, group_rows, 1)
        key_doc = lax.dynamic_slice_in_dim(doc_full, row_start, group_rows, 1)
        key_pos = lax.dynamic_slice_in_dim(positions, row_start, group_rows, 1)
        live_pairs = live_mask(key_doc, key_pos)
        scores = scores_of(key_block)
        block_max = jnp.max(jnp.where(live_pairs, scores, NEG_FILL), axis=1)
        new_max = jnp.maximum(run_max, block_max)
        exp_terms = jnp.where(live_pairs, jnp.exp(scores - new_max[:, None, :]), 0.0)
        run_sum = run_sum * jnp.exp(run_max - new_max) + jnp.sum(exp_terms, axis=1)
        return (new_max, run_sum)

    start_max = jnp.full((seq_count, query_total), NEG_FILL, jnp.float32)
    start_sum = jnp.zeros((seq_count, query_total), jnp.float32)
    run_max, run_sum = lax.fori_loop(0, ctx_count // 4, stats_step, (start_max, start_sum))
    log_total = run_max + jnp.log(run_sum)

    def block_terms(row_start, block_rows):
        key_block = lax.dynamic_slice_in_dim(key_all, row_start, block_rows, 1)
        value_block = lax.dynamic_slice_in_dim(value_all, row_start, block_rows, 1)
        key_doc = lax.dynamic_slice_in_dim(doc_full, row_start, block_rows, 1)
        key_pos = lax.dynamic_slice_in_dim(positions, row_start, block_rows, 1)
        live_pairs = live_mask(key_doc, key_pos)
        scores = scores_of(key_block)
        probs = jnp.where(live_pairs, jnp.exp(scores - log_total[:, None, :]), 0.0)
        probs_half = probs.astype(jnp.bfloat16)
        value_grad = jnp.einsum(
            "skn,snd->skd", probs_half, grad_n, preferred_element_type=jnp.float32
        )
        prob_grad = jnp.einsum(
            "skd,snd->skn", value_block, grad_n, preferred_element_type=jnp.float32
        )
        score_grad = (probs * (prob_grad - delta_n[:, None, :])).astype(jnp.bfloat16)
        query_part = jnp.einsum(
            "skn,skd->snd", score_grad, key_block, preferred_element_type=jnp.float32
        )
        key_grad = (
            jnp.einsum("skn,snd->skd", score_grad, query_n, preferred_element_type=jnp.float32)
            * score_scale
        )
        return (jnp.concatenate([key_grad, value_grad], axis=2), query_part)

    start_query = jnp.zeros((seq_count, query_total, head_size), jnp.float32)

    def pass_on(accumulated):
        return passed_along(accumulated, "ctx", 1)

    def one_block(accumulated, query_sum, step_index):
        block_index = (ctx_index - step_index - 1) % ctx_count
        partial_value, query_part = block_terms(block_index * row_count, row_count)
        return (accumulated + partial_value, query_sum + query_part)

    def four_steps(turn_index, loop_state):
        accumulated, query_sum = loop_state
        for inner_step in range(4):
            accumulated, query_sum = one_block(accumulated, query_sum, 4 * turn_index + inner_step)
            accumulated = pass_on(accumulated)
        return (accumulated, query_sum)

    start_accum = jnp.zeros((seq_count, row_count, 2 * head_size), jnp.float32)
    accumulated, query_sum = lax.fori_loop(
        0, ctx_count // 4 - 1, four_steps, (start_accum, start_query)
    )
    for inner_step in range(3):
        accumulated, query_sum = one_block(accumulated, query_sum, ctx_count - 4 + inner_step)
        accumulated = pass_on(accumulated)
    accumulated, query_sum = one_block(accumulated, query_sum, ctx_count - 1)
    query_grad = (query_sum * score_scale).reshape(seq_count, head_count, row_count, head_size)
    query_grad = (
        query_grad.transpose(0, 2, 1, 3)
        .reshape(seq_count, row_count, head_count * head_size)
        .astype(jnp.bfloat16)
    )
    kv_half = accumulated.astype(jnp.bfloat16)
    flat_input = layer_input.reshape(seq_count * row_count, model_width)
    flat_grad = kv_half.reshape(seq_count * row_count, 2 * head_size)
    row_share = lax.psum_scatter(
        lax.dot_general(
            flat_input, flat_grad, (((0,), (0,)), ((), ())), preferred_element_type=jnp.float32
        ),
        "ctx",
        scatter_dimension=0,
        tiled=True,
    )
    weight_grad = lax.psum(row_share, "dp")
    return (query_grad, weight_grad)


def solution(mesh):
    in_specs = (
        P("dp", "ctx", None),
        P("dp", "ctx", None),
        P("dp", "ctx", None),
        P("dp", "ctx", None),
        P("dp", "ctx", None),
        P("dp", "ctx", None),
        P("dp", None),
        P("dp", None),
    )
    out_specs = (P("dp", "ctx", None), P("ctx", None))
    return jax.shard_map(local, mesh=mesh, in_specs=in_specs, out_specs=out_specs, check_vma=False)
```

profile of v0, /device:TPU:1, one launch (start us, length us, event | category | flops | bytes accessed | tf_op | source)
XLA Modules:
  0.0 2075.9 jit_solution(13382836654781288007)
XLA Ops:
  11.6 69.1 %gather_fusion = s32[8192]{0:T(1024)S(1)} fusion(s32[2,4096]{1,0:T(2,128)S(1)} %copy-done.1, s32[8192]{0:T(1024)S(1)} %bitcast.181), kind=kCustom, calls=%fused_computation | custom fusion | bytes 131072 | tf_op jit(solution)/shard_map/jit(take_along_axis)/gather | solution.py:39
  81.1 244.9 %all-gather.3.cloned.1.call-done = bf16[2,4096,128]{2,1,0:T(8,128)(2,1)} async-done(((bf16[2,64,128]{2,1,0:T(8,128)(2,1)}), bf16[2,4096,128]{2,1,0:T(8,128)(2,1)}) %all-gather.3.cloned.1.call-update) | async-done | bytes 2097168 | tf_op jit(solution)/shard_map/all_gather | solution.py:45
  326.0 30.1 %while.36 = (s32[]{:T(128)}, f32[2,512]{1,0:T(2,128)S(1)}, f32[2,512]{1,0:T(2,128)S(1)}, s32[2,4096]{1,0:T(2,128)S(1)}, s32[2,4096]{1,0:T(2,128)S(1)}, /*index=5...) while((s32[]{:T(128)}, f32[2,512]{1,0:T(2,128)S(1)}, ...), condition=%wide.region_3.4_spmd.clone, body=%wide.region_0.3_spmd.clone.sunk | while | flops 70259720 | bytes 2602182 | solution.py:78
  364.2 316.7 %all-gather.5.cloned.1.call-done = bf16[2,4096,128]{2,1,0:T(8,128)(2,1)} async-done(((bf16[2,64,128]{2,1,0:T(8,128)(2,1)}), bf16[2,4096,128]{2,1,0:T(8,128)(2,1)}) %all-gather.5.cloned.1.call-update) | async-done | bytes 2097168 | tf_op jit(solution)/shard_map/all_gather | solution.py:46
  682.7 754.8 %while.37 = (s32[]{:T(128)}, f32[2,64,256]{2,1,0:T(8,128)S(1)}, f32[2,512,128]{2,1,0:T(8,128)S(1)}, s32[]{:T(128)}, s32[2,4096]{1,0:T(2,128)S(1)}, /*index=5*/s3...) while((s32[]{:T(128)}, f32[2,64,256]{2,1,0:T(8,128)S(1)}, ...), condition=%wide.wide.region_6.7_spmd.clone, body=%wide.wide.region_5.6_spmd.clone.sunk | while | flops 339148864 | bytes 17799364 | solution.py:124
  711.2 9.7 collective-permute-done.2
  749.3 9.6 collective-permute-done.1
  761.0 9.6 collective-permute-done.2
  800.3 10.5 collective-permute-done.1
  900.6 9.6 collective-permute-done.1
  950.6 10.3 collective-permute-done.1
  1001.0 9.6 collective-permute-done.1
  1012.7 9.6 collective-permute-done.2
  1050.7 9.6 collective-permute-done.1
  1062.4 9.6 collective-permute-done.2
  1100.9 9.7 collective-permute-done.1
  1112.8 9.6 collective-permute-done.2
  1224.9 9.8 collective-permute-done.3
  1251.3 10.3 collective-permute-done.1
  1263.7 10.9 collective-permute-done.2
  1402.4 10.5 collective-permute-done.1
  1415.1 10.6 collective-permute-done.2
  1485.4 438.7 %reduce-scatter.4.cloned.1.call-done = f32[64,256]{1,0:T(8,128)} async-done(((f32[4096,256]{1,0:T(8,128)}), f32[64,256]{1,0:T(8,128)}) %reduce-scatter.4.cloned.1.call-update) | async-done | bytes 65552
  1927.5 140.3 %all-reduce.2.cloned.1.call-done = f32[64,256]{0,1:T(8,128)} async-done(((f32[64,256]{0,1:T(8,128)}), f32[64,256]{0,1:T(8,128)}) %all-reduce.2.cloned.1.call-update) | async-done | bytes 65552 | tf_op jit(solution)/shard_map/psum | solution.py:148
  (782 shorter events, 678.3 us)
Async XLA Ops:
  7.2 318.8 %all-gather.3.cloned.1.call-start = ((), (), s32[]{:S(2)}) async-start(), calls=%async_computation.1 | async-start | bytes 2129920 | tf_op jit(solution)/shard_map/all_gather | solution.py:45
  7.9 672.9 %all-gather.5.cloned.1.call-start = ((), (), s32[]{:S(2)}) async-start(), calls=%async_computation.2 | async-start | bytes 2129920 | tf_op jit(solution)/shard_map/all_gather | solution.py:46
  8.7 1915.4 %reduce-scatter.4.cloned.1.call-start = ((), (), s32[]{:S(2)}) async-start(), calls=%async_computation.4 | async-start | bytes 4259840
  685.4 11.8 collective-permute-start
  709.1 11.8 collective-permute-start.2
  735.3 11.8 collective-permute-start
  785.1 13.0 collective-permute-start
  798.2 12.6 collective-permute-start.1
  836.9 11.8 collective-permute-start
  886.6 11.8 collective-permute-start
  922.0 12.0 collective-permute-start.3
  948.5 12.4 collective-permute-start.1
  1072.1 12.3 collective-permute-start.3
  1098.8 11.9 collective-permute-start.1
  1186.5 11.8 collective-permute-start
  1221.9 12.8 collective-permute-start.3
  1249.2 12.4 collective-permute-start.1
  1261.6 13.0 collective-permute-start.2
  1338.7 11.8 collective-permute-start
  1388.4 11.8 collective-permute-start
  1400.3 12.6 collective-permute-start.1
  1413.0 12.8 collective-permute-start.2
  1438.4 11.9 collective-permute-start.4
  1482.1 585.6 %all-reduce.2.cloned.1.call-start = ((), (), s32[]{:S(2)}) async-start(), calls=%async_computation.3 | async-start | bytes 262144 | tf_op jit(solution)/shard_map/psum | solution.py:148
  (53 other events, 2201.5 us)
Sparse Core Ops, SparseCore 0:
  10.1 315.8 all-gather.2
  328.1 352.7 all-gather.4
  1482.3 441.7 reduce-scatter.3
  1927.1 140.6 all-reduce.1
where the time goes:
time: 2090 us; the launch traced here: 2080 us
  waiting for transfers between devices  1600 us (77%)
  matrix products  243 us (12%)
  starting transfers between devices  121 us (6%)
  local copies, waits for them, and re-layouts  86.8 us (4%)
    ppermute x63, waiting for transfers between devices, passed_along(): lax.ppermute(x, axis, [(i, (i + by) % length) for i in range(length)])  454 us
    unnamed x5, waiting for transfers between devices  440 us
    all_gather x1, waiting for transfers between devices, local(): lax.all_gather(value_states, 'ctx', axis=1, tiled=True)  317 us
    all_gather x1, waiting for transfers between devices, local(): lax.all_gather(key_states, 'ctx', axis=1, tiled=True)  245 us
    psum x1, waiting for transfers between devices, local(): weight_grad = lax.psum(row_share, 'dp')  140 us
    ppermute x63, starting transfers between devices, passed_along(): lax.ppermute(x, axis, [(i, (i + by) % length) for i in range(length)])  121 us
    dot_general x80, matrix products, scores_of(): jnp.einsum('skd,snd->skn', key_block, query_n, preferred_element_type=jnp...  84.8 us
    gather x2, local copies, waits for them, and re-layouts, local(): doc_full = jnp.take_along_axis(doc_ids, positions, axis=1)  69.1 us
  transfers between devices with their start and end apart: 67, of which 53 were waited for; matrix products, arithmetic and copies ran while one was open for 14% of the time, Pallas kernels for 0%

commit v1 on v0

--- a/solution.py
+++ b/solution.py
@@ -43,7 +43,9 @@
     query_doc = jnp.tile(own_doc, (1, head_count))
     key_all, value_all = (
         lax.all_gather(key_states, "ctx", axis=1, tiled=True),
-        lax.all_gather(value_states, "ctx", axis=1, tiled=True),
+        jnp.concatenate(
+            lax.all_to_all(jnp.stack([value_states] * lax.axis_size("ctx")), "ctx", 0, 0), axis=1
+        ),
     )
     group_rows = 4 * row_count
     query_total = head_count * row_count

time: 2090 us -> 1810 us (0.87)
  waiting for transfers between devices: 1600 us -> 1270 us
  local copies, waits for them, and re-layouts: 86.8 us -> 122 us
    all_gather x1 -> x0, waiting for transfers between devices: 317 us -> none  [local(): lax.all_gather(value_states, 'ctx', axis=1, tiled=True)]
    unnamed x5 -> x4, waiting for transfers between devices: 440 us -> 438 us
  transfers between devices with their start and end apart: 67 -> 67, of which waited for: 53 -> 51; matrix products, arithmetic and copies ran while one was open for 14% -> 16% of each run, Pallas kernels for 0% -> 0%
where the time goes in v1:
time: 1810 us; the launch traced here: 1790 us
  waiting for transfers between devices  1270 us (70%)
  matrix products  239 us (13%)
  starting transfers between devices  135 us (7%)
  local copies, waits for them, and re-layouts  122 us (7%)
    ppermute x63, waiting for transfers between devices, passed_along(): lax.ppermute(x, axis, [(i, (i + by) % length) for i in range(length)])  459 us
    unnamed x4, waiting for transfers between devices  438 us
    all_gather x1, waiting for transfers between devices, local(): lax.all_gather(key_states, 'ctx', axis=1, tiled=True)  232 us
    psum x1, waiting for transfers between devices, local(): weight_grad = lax.psum(row_share, 'dp')  139 us
    ppermute x63, starting transfers between devices, passed_along(): lax.ppermute(x, axis, [(i, (i + by) % length) for i in range(length)])  122 us
    dot_general x80, matrix products, scores_of(): jnp.einsum('skd,snd->skn', key_block, query_n, preferred_element_type=jnp...  84.7 us
    gather x2, local copies, waits for them, and re-layouts, local(): doc_full = jnp.take_along_axis(doc_ids, positions, axis=1)  69.1 us
    dot_general x64, matrix products, block_terms(): jnp.einsum('skn,skd->snd', score_grad, key_block, preferred_element_type=...  67.1 us
  transfers between devices with their start and end apart: 67, of which 51 were waited for; matrix products, arithmetic and copies ran while one was open for 16% of the time, Pallas kernels for 0%

profile of v1, /device:TPU:1, one launch (start us, length us, event | category | flops | bytes accessed | tf_op | source)
XLA Modules:
  0.0 1794.1 jit_solution(5832463960063256855)
XLA Ops:
  10.5 12.9 all-to-all-start
  24.4 69.1 %gather_fusion = s32[8192]{0:T(1024)S(1)} fusion(s32[2,4096]{1,0:T(2,128)S(1)} %copy-done.1, s32[8192]{0:T(1024)S(1)} %bitcast.186), kind=kCustom, calls=%fused_computation | custom fusion | bytes 131072 | tf_op jit(solution)/shard_map/jit(take_along_axis)/gather | solution.py:39
  95.4 232.3 %all-gather.2.cloned.1.call-done = bf16[2,4096,128]{2,1,0:T(8,128)(2,1)} async-done(((bf16[2,64,128]{2,1,0:T(8,128)(2,1)}), bf16[2,4096,128]{2,1,0:T(8,128)(2,1)}) %all-gather.2.cloned.1.call-update) | async-done | bytes 2097168 | tf_op jit(solution)/shard_map/all_gather | solution.py:45
  327.7 40.7 %while.36 = (s32[]{:T(128)}, f32[2,512]{1,0:T(2,128)S(1)}, f32[2,512]{1,0:T(2,128)S(1)}, s32[2,4096]{1,0:T(2,128)}, s32[2,4096]{1,0:T(2,128)S(1)}, /*index=5*/bf...) while((s32[]{:T(128)}, f32[2,512]{1,0:T(2,128)S(1)}, ...), condition=%wide.region_3.4_spmd.clone, body=%wide.region_0.3_spmd.clone.sunk | while | flops 70259720 | bytes 2602182 | solution.py:80
  379.1 776.3 %while.37 = (s32[]{:T(128)}, f32[2,64,256]{2,1,0:T(8,128)S(1)}, f32[2,512,128]{2,1,0:T(8,128)S(1)}, s32[]{:T(128)}, s32[2,4096]{1,0:T(2,128)}, /*index=5*/s32[2,...) while((s32[]{:T(128)}, f32[2,64,256]{2,1,0:T(8,128)S(1)}, ...), condition=%wide.wide.region_6.7_spmd.clone, body=%wide.wide.region_5.6_spmd.clone.sunk | while | flops 339148864 | bytes 17816800 | solution.py:126
  449.1 9.6 collective-permute-done.1
  460.8 9.6 collective-permute-done.2
  500.1 10.2 collective-permute-done.1
  512.5 11.0 collective-permute-done.2
  553.7 9.6 collective-permute-done.1
  616.4 9.6 collective-permute-done.2
  655.7 10.1 collective-permute-done.1
  668.0 11.1 collective-permute-done.2
  709.2 9.6 collective-permute-done.1
  760.2 9.6 collective-permute-done.1
  823.0 11.1 collective-permute-done.2
  864.4 10.1 collective-permute-done.1
  915.9 9.6 collective-permute-done.1
  927.6 9.6 collective-permute-done.2
  1018.3 10.3 collective-permute-done.1
  1030.7 10.9 collective-permute-done.2
  1071.3 9.6 collective-permute-done.1
  1205.6 437.7 %reduce-scatter.4.cloned.1.call-done = f32[64,256]{1,0:T(8,128)} async-done(((f32[4096,256]{1,0:T(8,128)}), f32[64,256]{1,0:T(8,128)}) %reduce-scatter.4.cloned.1.call-update) | async-done | bytes 65552
  1646.7 139.3 %all-reduce.2.cloned.1.call-done = f32[64,256]{0,1:T(8,128)} async-done(((f32[64,256]{0,1:T(8,128)}), f32[64,256]{0,1:T(8,128)}) %all-reduce.2.cloned.1.call-update) | async-done | bytes 65552 | tf_op jit(solution)/shard_map/psum | solution.py:150
  (813 shorter events, 712.9 us)
Async XLA Ops:
  7.2 320.5 %all-gather.2.cloned.1.call-start = ((), (), s32[]{:S(2)}) async-start(), calls=%async_computation.2 | async-start | bytes 2129920 | tf_op jit(solution)/shard_map/all_gather | solution.py:45
  10.5 365.1 %all-to-all-start = ((bf16[64,2,64,128]{3,2,1,0:T(8,128)(2,1)}), bf16[64,2,64,128]{3,2,1,0:T(8,128)(2,1)}, u32[]{:S(2)}, u32[]{:S(2)}) async-start(bf16[64,2,64,128]{3,2,1,0:T(8,128)(2,1)} %stack.2), calls=%async_computation | async-start | bytes 4194304 | tf_op jit(solution)/shard_map/all_to_all | solution.py:47
  23.5 1619.8 %reduce-scatter.4.cloned.1.call-start = ((), (), s32[]{:S(2)}) async-start(), calls=%async_computation.4 | async-start | bytes 4259840
  383.1 12.8 collective-permute-start
  498.0 12.3 collective-permute-start.1
  510.4 13.1 collective-permute-start.2
  523.5 12.2 collective-permute-start.3
  539.7 11.8 collective-permute-start
  590.7 11.8 collective-permute-start
  653.6 12.2 collective-permute-start.1
  665.8 13.2 collective-permute-start.2
  679.0 12.3 collective-permute-start.3
  797.3 11.8 collective-permute-start
  820.9 13.2 collective-permute-start.2
  834.1 12.3 collective-permute-start.3
  850.4 11.8 collective-permute-start
  862.3 12.2 collective-permute-start.1
  901.9 11.8 collective-permute-start
  952.9 11.8 collective-permute-start
  988.3 12.1 collective-permute-start.3
  1016.2 12.4 collective-permute-start.1
  1028.6 13.0 collective-permute-start.2
  1108.3 11.8 collective-permute-start
  1201.6 584.4 %all-reduce.2.cloned.1.call-start = ((), (), s32[]{:S(2)}) async-start(), calls=%async_computation.3 | async-start | bytes 262144 | tf_op jit(solution)/shard_map/psum | solution.py:150
  (68 other events, 1982.6 us)
Sparse Core Ops, SparseCore 0:
  10.1 317.5 all-gather.1
  1201.7 441.5 reduce-scatter.3
  1646.4 139.5 all-reduce.1

commit v2 on v0

--- a/solution.py
+++ b/solution.py
@@ -145,7 +145,7 @@
         scatter_dimension=0,
         tiled=True,
     )
-    weight_grad = lax.psum(row_share, "dp")
+    weight_grad = jnp.sum(lax.all_gather(row_share, "dp"), axis=0)
     return (query_grad, weight_grad)
 
 

time: 2090 us -> 2020 us (0.967)
  waiting for transfers between devices: 1600 us -> 1450 us
  blocking collectives: 0 us -> 72.5 us
    unnamed x5 -> x3, waiting for transfers between devices: 440 us -> 1.39 us
    reduce_scatter x0 -> x1, waiting for transfers between devices: none -> 437 us  [local(): lax.psum_scatter(lax.dot_general(flat_input, flat_grad, (((0,), (0,)), ((...]
    psum x1 -> x0, waiting for transfers between devices: 140 us -> none  [local(): weight_grad = lax.psum(row_share, 'dp')]
    all_gather x0 -> x1, blocking collectives: none -> 72.5 us  [local(): weight_grad = jnp.sum(lax.all_gather(row_share, 'dp'), axis=0)]
  transfers between devices with their start and end apart: 67 -> 66, of which waited for: 53 -> 52; matrix products, arithmetic and copies ran while one was open for 14% -> 14% of each run, Pallas kernels for 0% -> 0%
where the time goes in v2:
time: 2020 us; the launch traced here: 2000 us
  waiting for transfers between devices  1450 us (72%)
  matrix products  243 us (12%)
  starting transfers between devices  121 us (6%)
  local copies, waits for them, and re-layouts  83.7 us (4%)
  blocking collectives  72.5 us (4%)
    ppermute x63, waiting for transfers between devices, passed_along(): lax.ppermute(x, axis, [(i, (i + by) % length) for i in range(length)])  455 us
    reduce_scatter x1, waiting for transfers between devices, local(): lax.psum_scatter(lax.dot_general(flat_input, flat_grad, (((0,), (0,)), ((...  437 us
    all_gather x1, waiting for transfers between devices, local(): lax.all_gather(value_states, 'ctx', axis=1, tiled=True)  317 us
    all_gather x1, waiting for transfers between devices, local(): lax.all_gather(key_states, 'ctx', axis=1, tiled=True)  245 us
    ppermute x63, starting transfers between devices, passed_along(): lax.ppermute(x, axis, [(i, (i + by) % length) for i in range(length)])  121 us
    dot_general x80, matrix products, scores_of(): jnp.einsum('skd,snd->skn', key_block, query_n, preferred_element_type=jnp...  84.8 us
    all_gather x1, blocking collectives, local(): weight_grad = jnp.sum(lax.all_gather(row_share, 'dp'), axis=0)  72.5 us
    gather x2, local copies, waits for them, and re-layouts, local(): doc_full = jnp.take_along_axis(doc_ids, positions, axis=1)  69.2 us
  transfers between devices with their start and end apart: 66, of which 52 were waited for; matrix products, arithmetic and copies ran while one was open for 14% of the time, Pallas kernels for 0%

profile of v2, /device:TPU:1, one launch (start us, length us, event | category | flops | bytes accessed | tf_op | source)
XLA Modules:
  0.0 2004.4 jit_solution(6655743280616031430)
XLA Ops:
  11.6 69.2 %gather_fusion = s32[8192]{0:T(1024)S(1)} fusion(s32[2,4096]{1,0:T(2,128)S(1)} %copy-done.1, s32[8192]{0:T(1024)S(1)} %bitcast.182), kind=kCustom, calls=%fused_computation | custom fusion | bytes 131072 | tf_op jit(solution)/shard_map/jit(take_along_axis)/gather | solution.py:39
  81.2 244.8 %all-gather.4.cloned.1.call-done = bf16[2,4096,128]{2,1,0:T(8,128)(2,1)} async-done(((bf16[2,64,128]{2,1,0:T(8,128)(2,1)}), bf16[2,4096,128]{2,1,0:T(8,128)(2,1)}) %all-gather.4.cloned.1.call-update) | async-done | bytes 2097168 | tf_op jit(solution)/shard_map/all_gather | solution.py:45
  326.0 30.2 %while.36 = (s32[]{:T(128)}, f32[2,512]{1,0:T(2,128)S(1)}, f32[2,512]{1,0:T(2,128)S(1)}, s32[2,4096]{1,0:T(2,128)S(1)}, s32[2,4096]{1,0:T(2,128)S(1)}, /*index=5...) while((s32[]{:T(128)}, f32[2,512]{1,0:T(2,128)S(1)}, ...), condition=%wide.region_3.4_spmd.clone, body=%wide.region_0.3_spmd.clone.sunk | while | flops 70259720 | bytes 2602182 | solution.py:78
  364.1 316.8 %all-gather.6.cloned.1.call-done = bf16[2,4096,128]{2,1,0:T(8,128)(2,1)} async-done(((bf16[2,64,128]{2,1,0:T(8,128)(2,1)}), bf16[2,4096,128]{2,1,0:T(8,128)(2,1)}) %all-gather.6.cloned.1.call-update) | async-done | bytes 2097168 | tf_op jit(solution)/shard_map/all_gather | solution.py:46
  682.7 755.2 %while.37 = (s32[]{:T(128)}, f32[2,64,256]{2,1,0:T(8,128)S(1)}, f32[2,512,128]{2,1,0:T(8,128)S(1)}, s32[]{:T(128)}, s32[2,4096]{1,0:T(2,128)S(1)}, /*index=5*/s3...) while((s32[]{:T(128)}, f32[2,64,256]{2,1,0:T(8,128)S(1)}, ...), condition=%wide.wide.region_6.7_spmd.clone, body=%wide.wide.region_5.6_spmd.clone.sunk | while | flops 339148864 | bytes 17799364 | solution.py:124
  711.2 9.7 collective-permute-done.2
  800.6 10.5 collective-permute-done.1
  851.1 9.6 collective-permute-done.1
  862.9 9.6 collective-permute-done.2
  900.8 9.6 collective-permute-done.1
  950.8 10.2 collective-permute-done.1
  1001.1 9.6 collective-permute-done.1
  1050.8 9.6 collective-permute-done.1
  1101.1 9.9 collective-permute-done.1
  1151.1 9.6 collective-permute-done.1
  1162.8 9.6 collective-permute-done.2
  1225.2 10.1 collective-permute-done.3
  1251.8 10.3 collective-permute-done.1
  1264.3 10.9 collective-permute-done.2
  1303.5 9.6 collective-permute-done.1
  1402.9 10.6 collective-permute-done.1
  1415.6 10.6 collective-permute-done.2
  1487.6 437.1 %reduce-scatter.4.cloned.1.call-done = f32[64,256]{1,0:T(8,128)} async-done(((f32[4096,256]{1,0:T(8,128)}), f32[64,256]{1,0:T(8,128)}) %reduce-scatter.4.cloned.1.call-update) | async-done | bytes 65552 | tf_op jit(solution)/shard_map/reduce_scatter | solution.py:140
  1924.7 72.5 %all-gather = f32[512,256]{1,0:T(8,128)S(1)} all-gather(f32[64,256]{1,0:T(8,128)} %reduce-scatter.4.cloned.1.call-done), channel_id=2, replica_groups=mesh['ctx'=64,'dp'=8] {'dp'}, dimensions={0}, use_global_device_ids=true | all-gather | bytes 589824 | tf_op jit(solution)/shard_map/all_gather | solution.py:148
  (779 shorter events, 675.8 us)
Async XLA Ops:
  7.2 318.8 %all-gather.4.cloned.1.call-start = ((), (), s32[]{:S(2)}) async-start(), calls=%async_computation.1 | async-start | bytes 2129920 | tf_op jit(solution)/shard_map/all_gather | solution.py:45
  7.9 673.0 %all-gather.6.cloned.1.call-start = ((), (), s32[]{:S(2)}) async-start(), calls=%async_computation.2 | async-start | bytes 2129920 | tf_op jit(solution)/shard_map/all_gather | solution.py:46
  8.7 1916.0 %reduce-scatter.4.cloned.1.call-start = ((), (), s32[]{:S(2)}) async-start(), calls=%async_computation.3 | async-start | bytes 4259840 | tf_op jit(solution)/shard_map/reduce_scatter | solution.py:140
  709.1 11.8 collective-permute-start.2
  770.6 11.9 collective-permute-start.3
  785.2 13.2 collective-permute-start
  798.4 12.6 collective-permute-start.1
  886.8 11.8 collective-permute-start
  922.2 12.1 collective-permute-start.3
  948.7 12.3 collective-permute-start.1
  1036.8 11.8 collective-permute-start
  1072.2 12.4 collective-permute-start.3
  1087.2 11.8 collective-permute-start
  1099.0 12.0 collective-permute-start.1
  1137.1 11.8 collective-permute-start
  1186.8 11.8 collective-permute-start
  1222.2 13.1 collective-permute-start.3
  1249.7 12.4 collective-permute-start.1
  1262.2 13.0 collective-permute-start.2
  1339.2 11.8 collective-permute-start
  1388.9 11.8 collective-permute-start
  1400.8 12.7 collective-permute-start.1
  1413.5 12.7 collective-permute-start.2
  1438.9 11.9 collective-permute-start.4
  (52 other events, 2190.0 us)
Sparse Core Ops, SparseCore 0:
  10.1 315.8 all-gather.3
  328.1 352.7 all-gather.5
  1482.7 441.9 reduce-scatter.3
